TPU v7x, 32 devices: a whole 2x2x4 slice. The times are simulated.
32 devices in a mesh: dp: 2 (over y), expert: 16 (over z, x, core).
Axes of the slice: x: 2, y: 2, z: 4, core: 2. Of those that a mesh axis runs over, the one named last changes fastest.
Arguments:
- tokens: bfloat16 [2048, 3584], P('expert', 'dp'), may hold values from -6 to 6
- expert_ids: int32 [2048, 8], P('expert'), may hold values from 0 to 63, all different within a row; in each aligned block of 128 rows (0 to 127, 128 to 255, ...) at most 32 rows name the same one
- gate_weight: float32 [2048, 8], P('expert'), may hold values from 0.1 to 0.6
- w_gate: bfloat16 [16, 3584, 1024], P('expert', 'dp'), may hold values from -0.09375 to 0.09375
- w_up: bfloat16 [16, 3584, 1024], P('expert', 'dp'), may hold values from -0.09375 to 0.09375
- w_down: bfloat16 [16, 1024, 3584], P('expert', None, 'dp'), may hold values from -0.1875 to 0.1875
- grad_out: bfloat16 [2048, 3584], P('expert', 'dp'), may hold values from -6 to 6
Outputs:
- output: bfloat16 [2048, 3584], P('expert', 'dp')
- grad_tokens: bfloat16 [2048, 3584], P('expert', 'dp')
- grad_down: bfloat16 [16, 1024, 3584], P('expert', None, 'dp')
Inputs may be any that keep to these rules, and one draw needn't show every extreme that they name: `expert_ids`: each row names 8 different experts. Among the rows of one device no expert is named by more than 32 rows, and in some device's rows some expert is named by exactly 32 rows.
All inputs are finite; a program needn't handle non-finite values.
Results may differ from a plain program's by a relative error of at most 0.024.
Values may be sent and summed in bfloat16 or wider, within the bound.
A program may use at most 64 MiB of HBM per device.

v0:
```python
import jax
import jax.numpy as jnp
from jax import lax
from jax.sharding import PartitionSpec as P


def local(tokens, expert_ids, gate_weight, w_gate, w_up, w_down, grad_out):
    tok_dev, fanout = expert_ids.shape
    feature_cols = tokens.shape[1]
    experts = lax.axis_size("expert")
    capacity = max(2, min(tok_dev, 2 * tok_dev * fanout // (4 * experts)))
    pair_count = tok_dev * fanout
    flat_ids = expert_ids.reshape(pair_count)
    onehot = (flat_ids[:, None] == jnp.arange(experts, dtype=jnp.int32)[None, :]).astype(jnp.int32)
    before = jnp.cumsum(onehot, axis=0) - onehot
    slot_index = jnp.sum(before * onehot, axis=1)
    position = flat_ids * capacity + slot_index
    placing = jnp.arange(experts * capacity, dtype=jnp.int32)[:, None] == position[None, :]
    placing = placing.reshape(experts * capacity, tok_dev, fanout)
    select = jnp.sum(placing.astype(jnp.float32), axis=2).astype(jnp.bfloat16)
    slot_gate = jnp.sum(jnp.where(placing, gate_weight[None, :, :], 0.0), axis=(1, 2))
    x_slab = jnp.dot(select, tokens, preferred_element_type=jnp.float32).astype(jnp.bfloat16)
    x_slab = x_slab.reshape(experts, capacity, feature_cols)
    cot_rows = jnp.dot(select, grad_out, preferred_element_type=jnp.float32)
    c_slab = (slot_gate[:, None] * cot_rows).astype(jnp.bfloat16)
    c_slab = c_slab.reshape(experts, capacity, feature_cols)
    gate_mat = w_gate[0]
    up_mat = w_up[0]
    down_mat = w_down[0]
    row_total = experts * capacity
    transposed = (((1,), (1,)), ((), ()))
    arrived = lax.all_to_all(x_slab, "expert", split_axis=0, concat_axis=0, tiled=True)
    x_rows = arrived.reshape(row_total, feature_cols)
    gate_part = jnp.dot(x_rows, gate_mat, preferred_element_type=jnp.float32)
    up_part = jnp.dot(x_rows, up_mat, preferred_element_type=jnp.float32)
    gate_pre = lax.psum(gate_part.astype(jnp.bfloat16), "dp").astype(jnp.float32)
    up_pre = lax.psum(up_part.astype(jnp.bfloat16), "dp").astype(jnp.float32)
    hidden = (jax.nn.silu(gate_pre) * up_pre).astype(jnp.bfloat16)
    out_rows = jnp.dot(hidden, down_mat, preferred_element_type=jnp.float32).astype(jnp.bfloat16)
    gate_pre, up_pre, hidden, out_rows = (
        gate_pre,
        up_pre,
        hidden,
        out_rows.reshape(experts, capacity, feature_cols),
    )
    back_out = lax.all_to_all(out_rows, "expert", split_axis=0, concat_axis=0, tiled=True)
    arrived_grads = lax.all_to_all(c_slab, "expert", split_axis=0, concat_axis=0, tiled=True)
    c_rows = arrived_grads.reshape(row_total, feature_cols)
    hidden_part = lax.dot_general(c_rows, down_mat, transposed, preferred_element_type=jnp.float32)
    sig = jax.nn.sigmoid(gate_pre)
    grad_hidden = lax.psum(hidden_part.astype(jnp.bfloat16), "dp").astype(jnp.float32)
    grad_gate = (grad_hidden * up_pre * sig * (1.0 + gate_pre * (1.0 - sig))).astype(jnp.bfloat16)
    grad_up = (grad_hidden * jax.nn.silu(gate_pre)).astype(jnp.bfloat16)
    grad_rows = lax.dot_general(grad_gate, gate_mat, transposed, preferred_element_type=jnp.float32)
    grad_rows = grad_rows + lax.dot_general(
        grad_up, up_mat, transposed, preferred_element_type=jnp.float32
    )
    grad_rows = grad_rows.astype(jnp.bfloat16).reshape(experts, capacity, feature_cols)
    down_grad = lax.dot_general(
        hidden, c_rows, (((0,), (0,)), ((), ())), preferred_element_type=jnp.float32
    )
    grad_rows, down_grad = (grad_rows, down_grad.astype(jnp.bfloat16))
    back_grads = lax.all_to_all(grad_rows, "expert", split_axis=0, concat_axis=0, tiled=True)
    scaled = back_out.reshape(row_total, feature_cols).astype(jnp.float32) * slot_gate[:, None]
    upper_part = scaled.astype(jnp.bfloat16)
    lower_part = (scaled - upper_part.astype(jnp.float32)).astype(jnp.bfloat16)
    output = jnp.dot(select.T, upper_part, preferred_element_type=jnp.float32)
    output = (output + jnp.dot(select.T, lower_part, preferred_element_type=jnp.float32)).astype(
        jnp.bfloat16
    )
    grad_flat = back_grads.reshape(row_total, feature_cols)
    grad_tokens = jnp.dot(select.T, grad_flat, preferred_element_type=jnp.float32).astype(
        jnp.bfloat16
    )
    return (output, grad_tokens, down_grad.reshape(1, down_grad.shape[0], feature_cols))


def solution(mesh):
    return jax.shard_map(
        local,
        mesh=mesh,
        in_specs=(
            P("expert", "dp"),
            P("expert", None),
            P("expert", None),
            P("expert", "dp", None),
            P("expert", "dp", None),
            P("expert", None, "dp"),
            P("expert", "dp"),
        ),
        out_specs=(P("expert", "dp"), P("expert", "dp"), P("expert", None, "dp")),
        check_vma=False,
    )
```

profile of v0, /device:TPU:11, one launch (start us, length us, event | category | flops | bytes accessed | tf_op | source)
XLA Modules:
  0.0 318.3 jit_solution(14854506770356374318)
XLA Ops:
  7.2 0.8 copy.28
  8.0 0.1 eq.44
  8.1 0.1 eq.40
  8.2 4.5 %reduce-window.6 = s32[16,8,128]{2,1,0:T(8,128)S(1)} reduce-window(s32[16,8,128]{2,1,0:T(8,128)S(1)} %fusion.48, s32[]{:T(128)} %constant.12.clone.1), window={size=1x1x128 pad=0_0x0_0x127_0}, to_apply=%region_0.0 | reduce-window | flops 2080768 | bytes 131076 | tf_op jit(solution)/shard_map/reduce-window
  12.8 0.1 copy.30
  13.1 0.1 broadcast_add_fusion
  13.3 0.7 multiply_add_fusion
  14.0 2.3 select_reduce_fusion
  16.4 1.9 convolution_convert_fusion.1
  18.3 6.7 %all-to-all-start = ((bf16[16,32,1792]{2,1,0:T(8,128)(2,1)}), bf16[16,32,1792]{2,1,0:T(8,128)(2,1)S(1)}, u32[]{:S(2)}, u32[]{:S(2)}) async-start(bf16[16,32,1792]{2,1,0:T(8,128)(2,1)} %bitcast.2), calls=%async_computation | async-start | bytes 3670016 | tf_op jit(solution)/shard_map/all_to_all | solution.py:32
  24.9 1.9 multiply_convert_fusion
  26.8 39.9 %all-to-all-done = bf16[16,32,1792]{2,1,0:T(8,128)(2,1)S(1)} async-done(((bf16[16,32,1792]{2,1,0:T(8,128)(2,1)}), bf16[16,32,1792]{2,1,0:T(8,128)(2,1)S(1)}, u32[]{:S(2)}, u32[]{:S(2)}) %all-to-all-start) | async-done | bytes 1835040 | tf_op jit(solution)/shard_map/all_to_all | solution.py:32
  66.7 1.2 copy-done.4
  67.9 4.8 %all-to-all-start.2 = ((bf16[16,32,1792]{2,1,0:T(8,128)(2,1)}), bf16[16,32,1792]{2,1,0:T(8,128)(2,1)S(1)}, u32[]{:S(2)}, u32[]{:S(2)}) async-start(bf16[16,32,1792]{2,1,0:T(8,128)(2,1)} %bitcast.9), calls=%async_computation.2 | async-start | bytes 3670016 | tf_op jit(solution)/shard_map/all_to_all | solution.py:47
  72.8 5.8 %fusion.36 = bf16[512,1024]{1,0:T(8,128)(2,1)} fusion(bf16[512,1792]{1,0:T(8,128)(2,1)} %bitcast.71, bf16[1,1792,1024]{2,1,0:T(8,128)(2,1)} %param.11), kind=kOutput, calls=%fused_computation.45 | convolution fusion | flops 1879572480 | bytes 6553600 | tf_op jit(solution)/shard_map/dot_general | solution.py:35
  78.6 3.0 fusion.33
  81.6 32.9 %all-to-all-done.2 = bf16[16,32,1792]{2,1,0:T(8,128)(2,1)S(1)} async-done(((bf16[16,32,1792]{2,1,0:T(8,128)(2,1)}), bf16[16,32,1792]{2,1,0:T(8,128)(2,1)S(1)}, u32[]{:S(2)}, u32[]{:S(2)}) %all-to-all-start.2) | async-done | bytes 1835040 | tf_op jit(solution)/shard_map/all_to_all | solution.py:47
  114.5 5.8 %fusion.39 = bf16[512,1024]{1,0:T(8,128)(2,1)} fusion(bf16[512,1792]{1,0:T(8,128)(2,1)S(1)} %bitcast.69, bf16[1,1024,1792]{2,1,0:T(8,128)(2,1)} %param.12), kind=kOutput, calls=%fused_computation.46 | convolution fusion | flops 1879572480 | bytes 6553600 | tf_op jit(solution)/shard_map/dot_general | solution.py:49
  120.3 85.3 %all-reduce.3.cloned.1.call-done = (bf16[512,1024]{1,0:T(8,128)(2,1)}, bf16[512,1024]{1,0:T(8,128)(2,1)}, bf16[512,1024]{1,0:T(8,128)(2,1)}) async-done(((bf16[512,1024]{1,0:T(8,128)(2,1)}, bf16[512,1024]{1,0:T(8,128)(2,1)}, bf16[512,1024]{1,0:T(8,128)(2,1)}), (bf16[512,1024]{1,0:T(8,128)(2,1)}, bf16[512,1024]{1,0:T(8,128)(2,1)}, bf16[512,1024]{1,0:T(8,128)(2,1)})) %all-reduce.3.cloned.1.call-update) | async-done | bytes 3145744 | tf_op jit(solution)/shard_map/psum | solution.py:37
  205.6 6.4 %fusion.18 = bf16[512,1792]{1,0:T(8,128)(2,1)} fusion(bf16[1,1024,1792]{2,1,0:T(8,128)(2,1)} %param.12, bf16[512,1024]{1,0:T(8,128)(2,1)} %get-tuple-element.5, bf16[512,1024]{1,0:T(8,128)(2,1)} %get-tuple-element.6), kind=kOutput, calls=%fused_computation.23 | convolution fusion | flops 1884160000 | bytes 7602176 | tf_op jit(solution)/shard_map/dot_general | solution.py:39
  212.0 6.5 %all-to-all-start.1 = ((bf16[16,32,1792]{2,1,0:T(8,128)(2,1)}), bf16[16,32,1792]{2,1,0:T(8,128)(2,1)S(1)}, u32[]{:S(2)}, u32[]{:S(2)}) async-start(bf16[16,32,1792]{2,1,0:T(8,128)(2,1)} %bitcast.74), calls=%async_computation.1 | async-start | bytes 3670016 | tf_op jit(solution)/shard_map/all_to_all | solution.py:46
  218.5 5.3 %fusion.7 = f32[512,1792]{1,0:T(8,128)S(1)} fusion(bf16[1,1792,1024]{2,1,0:T(8,128)(2,1)} %param.11, bf16[512,1024]{1,0:T(8,128)(2,1)} %get-tuple-element.7, bf16[512,1024]{1,0:T(8,128)(2,1)} %get-tuple-element.6), kind=kOutput, calls=%fused_computation.9 | convolution fusion | flops 1883242496 | bytes 9437184 | tf_op jit(solution)/shard_map/dot_general | solution.py:55
  223.8 4.2 %add_convert_fusion = bf16[512,1792]{1,0:T(8,128)(2,1)} fusion(f32[512,1792]{1,0:T(8,128)S(1)} %fusion.7, bf16[1,1792,1024]{2,1,0:T(8,128)(2,1)S(1)} %copy-done.8, bf16[512,1024]{1,0:T(8,128)(2,1)S(1)} %copy-done.9, bf16[512,1024]{1,0:T(8,128)(2,1)S(1)} %copy-done.11, bf16[512,1024]{1,0:T(8,128)(2,1)S(1)} %copy-done.10), kind=kOutput, calls=%fused_computation.17 | convolution fusion | flops 1887698944 | bytes 12320768 | tf_op jit(solution)/shard_map/dot_general | solution.py:54
  228.0 32.3 %all-to-all-done.1 = bf16[16,32,1792]{2,1,0:T(8,128)(2,1)S(1)} async-done(((bf16[16,32,1792]{2,1,0:T(8,128)(2,1)}), bf16[16,32,1792]{2,1,0:T(8,128)(2,1)S(1)}, u32[]{:S(2)}, u32[]{:S(2)}) %all-to-all-start.1) | async-done | bytes 1835040 | tf_op jit(solution)/shard_map/all_to_all | solution.py:46
  260.3 4.8 %all-to-all-start.3 = ((bf16[16,32,1792]{2,1,0:T(8,128)(2,1)}), bf16[16,32,1792]{2,1,0:T(8,128)(2,1)}, u32[]{:S(2)}, u32[]{:S(2)}) async-start(bf16[16,32,1792]{2,1,0:T(8,128)(2,1)} %bitcast.73), calls=%async_computation.3 | async-start | bytes 3670016 | tf_op jit(solution)/shard_map/all_to_all | solution.py:63
  265.0 6.2 %fusion.15 = bf16[1,1024,1792]{2,1,0:T(8,128)(2,1)} fusion(bf16[512,1792]{1,0:T(8,128)(2,1)} %bitcast.70, bf16[512,1024]{1,0:T(8,128)(2,1)} %get-tuple-element.5, bf16[512,1024]{1,0:T(8,128)(2,1)} %get-tuple-element.6), kind=kOutput, calls=%fused_computation.19 | convolution fusion | flops 1885077504 | bytes 7602176 | tf_op jit(solution)/shard_map/dot_general | solution.py:59
  271.3 0.4 fusion.1
  271.7 1.2 copy-done.1
  272.9 0.4 fusion.53
  273.3 33.6 %all-to-all-done.3 = bf16[16,32,1792]{2,1,0:T(8,128)(2,1)} async-done(((bf16[16,32,1792]{2,1,0:T(8,128)(2,1)}), bf16[16,32,1792]{2,1,0:T(8,128)(2,1)}, u32[]{:S(2)}, u32[]{:S(2)}) %all-to-all-start.3) | async-done | bytes 1835040 | tf_op jit(solution)/shard_map/all_to_all | solution.py:63
  306.9 2.8 convolution_convert_fusion.2
  309.8 1.7 fusion.21
  (32 shorter events, 0.4 us)
Async XLA Ops:
  7.2 9.2 %copy-start = (bf16[128,1792]{1,0:T(8,128)(2,1)S(1)}, bf16[128,1792]{1,0:T(8,128)(2,1)}, u32[]{:S(2)}) copy-start(bf16[128,1792]{1,0:T(8,128)(2,1)} %param.7) | copy-start | bytes 1376260
  18.2 6.7 %copy-start.6 = (bf16[128,1792]{1,0:T(8,128)(2,1)S(1)}, bf16[128,1792]{1,0:T(8,128)(2,1)}, u32[]{:S(2)}) copy-start(bf16[128,1792]{1,0:T(8,128)(2,1)} %param.13) | copy-start | bytes 1376260
  18.3 48.5 %all-to-all-start = ((bf16[16,32,1792]{2,1,0:T(8,128)(2,1)}), bf16[16,32,1792]{2,1,0:T(8,128)(2,1)S(1)}, u32[]{:S(2)}, u32[]{:S(2)}) async-start(bf16[16,32,1792]{2,1,0:T(8,128)(2,1)} %bitcast.2), calls=%async_computation | async-start | bytes 3670016 | tf_op jit(solution)/shard_map/all_to_all | solution.py:32
  66.7 1.2 copy-start.4
  67.9 46.6 %all-to-all-start.2 = ((bf16[16,32,1792]{2,1,0:T(8,128)(2,1)}), bf16[16,32,1792]{2,1,0:T(8,128)(2,1)S(1)}, u32[]{:S(2)}, u32[]{:S(2)}) async-start(bf16[16,32,1792]{2,1,0:T(8,128)(2,1)} %bitcast.9), calls=%async_computation.2 | async-start | bytes 3670016 | tf_op jit(solution)/shard_map/all_to_all | solution.py:47
  72.7 132.9 %all-reduce.3.cloned.1.call-start = ((), (), s32[]{:S(2)}) async-start(), calls=%async_computation.4 | async-start | bytes 6291456 | tf_op jit(solution)/shard_map/psum | solution.py:37
  72.8 5.8 %copy-start.5 = (bf16[16,32,1792]{2,1,0:T(8,128)(2,1)S(1)}, bf16[16,32,1792]{2,1,0:T(8,128)(2,1)}, u32[]{:S(2)}) copy-start(bf16[16,32,1792]{2,1,0:T(8,128)(2,1)} %copy-done.4) | copy-start | bytes 5505028
  72.8 5.8 %copy-start.7 = (bf16[1,1792,1024]{2,1,0:T(8,128)(2,1)S(1)}, bf16[1,1792,1024]{2,1,0:T(8,128)(2,1)}, u32[]{:S(2)}) copy-start(bf16[1,1792,1024]{2,1,0:T(8,128)(2,1)} %param.10) | copy-start | bytes 11010052
  114.5 5.8 %copy-start.3 = (bf16[16,32,1792]{2,1,0:T(8,128)(2,1)}, bf16[16,32,1792]{2,1,0:T(8,128)(2,1)S(1)}, u32[]{:S(2)}) copy-start(bf16[16,32,1792]{2,1,0:T(8,128)(2,1)S(1)} %all-to-all-done.2) | copy-start | bytes 5505028
  212.0 48.3 %all-to-all-start.1 = ((bf16[16,32,1792]{2,1,0:T(8,128)(2,1)}), bf16[16,32,1792]{2,1,0:T(8,128)(2,1)S(1)}, u32[]{:S(2)}, u32[]{:S(2)}) async-start(bf16[16,32,1792]{2,1,0:T(8,128)(2,1)} %bitcast.74), calls=%async_computation.1 | async-start | bytes 3670016 | tf_op jit(solution)/shard_map/all_to_all | solution.py:46
  218.5 5.3 %copy-start.8 = (bf16[1,1792,1024]{2,1,0:T(8,128)(2,1)S(1)}, bf16[1,1792,1024]{2,1,0:T(8,128)(2,1)}, u32[]{:S(2)}) copy-start(bf16[1,1792,1024]{2,1,0:T(8,128)(2,1)} %param.10) | copy-start | bytes 11010052
  218.5 5.3 %copy-start.9 = (bf16[512,1024]{1,0:T(8,128)(2,1)S(1)}, bf16[512,1024]{1,0:T(8,128)(2,1)}, u32[]{:S(2)}) copy-start(bf16[512,1024]{1,0:T(8,128)(2,1)} %get-tuple-element.5) | copy-start | bytes 3145732
  218.5 5.3 %copy-start.10 = (bf16[512,1024]{1,0:T(8,128)(2,1)S(1)}, bf16[512,1024]{1,0:T(8,128)(2,1)}, u32[]{:S(2)}) copy-start(bf16[512,1024]{1,0:T(8,128)(2,1)} %get-tuple-element.6) | copy-start | bytes 3145732
  218.5 5.3 %copy-start.11 = (bf16[512,1024]{1,0:T(8,128)(2,1)S(1)}, bf16[512,1024]{1,0:T(8,128)(2,1)}, u32[]{:S(2)}) copy-start(bf16[512,1024]{1,0:T(8,128)(2,1)} %get-tuple-element.7) | copy-start | bytes 3145732
  260.3 46.7 %all-to-all-start.3 = ((bf16[16,32,1792]{2,1,0:T(8,128)(2,1)}), bf16[16,32,1792]{2,1,0:T(8,128)(2,1)}, u32[]{:S(2)}, u32[]{:S(2)}) async-start(bf16[16,32,1792]{2,1,0:T(8,128)(2,1)} %bitcast.73), calls=%async_computation.3 | async-start | bytes 3670016 | tf_op jit(solution)/shard_map/all_to_all | solution.py:63
  271.7 1.2 copy-start.1
  306.9 2.8 copy-start.2
Sparse Core Ops, SparseCore 0:
  120.4 85.1 all-reduce.2
where the time goes:
time: 319 us; the launch traced here: 318 us
  waiting for transfers between devices  224 us (70%)
  matrix products  45.3 us (14%)
  starting transfers between devices  22.8 us (7%)
  between operations  14.2 us (4%)
  other arithmetic  8.11 us (3%)
  local copies, waits for them, and re-layouts  3.94 us (1%)
    psum x1, waiting for transfers between devices, local(): up_pre = lax.psum(up_part.astype(jnp.bfloat16), 'dp').astype(jnp.float32)  85.3 us
    all_to_all x1, waiting for transfers between devices, local(): lax.all_to_all(x_slab, 'expert', split_axis=0, concat_axis=0, tiled=True)  39.9 us
    all_to_all x1, waiting for transfers between devices, local(): lax.all_to_all(grad_rows, 'expert', split_axis=0, concat_axis=0, tiled=True)  33.6 us
    all_to_all x1, waiting for transfers between devices, local(): lax.all_to_all(c_slab, 'expert', split_axis=0, concat_axis=0, tiled=True)  32.9 us
    all_to_all x1, waiting for transfers between devices, local(): lax.all_to_all(out_rows, 'expert', split_axis=0, concat_axis=0, tiled=True)  32.3 us
    all_to_all x1, starting transfers between devices, local(): lax.all_to_all(x_slab, 'expert', split_axis=0, concat_axis=0, tiled=True)  6.65 us
    all_to_all x1, starting transfers between devices, local(): lax.all_to_all(out_rows, 'expert', split_axis=0, concat_axis=0, tiled=True)  6.51 us
  transfers between devices with their start and end apart: 5, of which 5 were waited for; matrix products, arithmetic and copies ran while one was open for 9% of the time, Pallas kernels for 0%

commit v1 on v0

--- a/solution.py
+++ b/solution.py
@@ -34,7 +34,7 @@
     gate_part = jnp.dot(x_rows, gate_mat, preferred_element_type=jnp.float32)
     up_part = jnp.dot(x_rows, up_mat, preferred_element_type=jnp.float32)
     gate_pre = lax.psum(gate_part.astype(jnp.bfloat16), "dp").astype(jnp.float32)
-    up_pre = lax.psum(up_part.astype(jnp.bfloat16), "dp").astype(jnp.float32)
+    up_pre = jnp.sum(lax.all_gather(up_part.astype(jnp.bfloat16), "dp"), axis=0).astype(jnp.float32)
     hidden = (jax.nn.silu(gate_pre) * up_pre).astype(jnp.bfloat16)
     out_rows = jnp.dot(hidden, down_mat, preferred_element_type=jnp.float32).astype(jnp.bfloat16)
     gate_pre, up_pre, hidden, out_rows = (

time: 319 us -> 332 us (1.041)
  waiting for transfers between devices: 224 us -> 231 us
  matrix products: 45.3 us -> 50.2 us
    psum x1, waiting for transfers between devices: 85.3 us -> 56.4 us  [local(): lax.psum(gate_part.astype(jnp.bfloat16), 'dp').astype(jnp.float32)]
    all_gather x0 -> x1, waiting for transfers between devices: none -> 27.7 us  [local(): lax.all_gather(up_part.astype(jnp.bfloat16), 'dp')]
    all_to_all x1, waiting for transfers between devices: 32.9 us -> 39.9 us  [local(): lax.all_to_all(c_slab, 'expert', split_axis=0, concat_axis=0, tiled=True)]
    dot_general x1, matrix products: 4.16 us -> 7.57 us  [local(): lax.dot_general(grad_gate, gate_mat, transposed, preferred_element_type=j...]
  transfers between devices with their start and end apart: 5 -> 6, of which waited for: 5 -> 6; matrix products, arithmetic and copies ran while one was open for 9% -> 10% of each run, Pallas kernels for 0% -> 0%
where the time goes in v1:
time: 332 us; the launch traced here: 331 us
  waiting for transfers between devices  231 us (70%)
  matrix products  50.2 us (15%)
  starting transfers between devices  23 us (7%)
  between operations  14.1 us (4%)
  other arithmetic  10.3 us (3%)
    psum x1, waiting for transfers between devices, local(): lax.psum(gate_part.astype(jnp.bfloat16), 'dp').astype(jnp.float32)  56.4 us
    all_to_all x1, waiting for transfers between devices, local(): lax.all_to_all(c_slab, 'expert', split_axis=0, concat_axis=0, tiled=True)  39.9 us
    all_to_all x1, waiting for transfers between devices, local(): lax.all_to_all(x_slab, 'expert', split_axis=0, concat_axis=0, tiled=True)  36.7 us
    all_to_all x1, waiting for transfers between devices, local(): lax.all_to_all(grad_rows, 'expert', split_axis=0, concat_axis=0, tiled=True)  35.7 us
    all_to_all x1, waiting for transfers between devices, local(): lax.all_to_all(out_rows, 'expert', split_axis=0, concat_axis=0, tiled=True)  34.6 us
    all_gather x1, waiting for transfers between devices, local(): lax.all_gather(up_part.astype(jnp.bfloat16), 'dp')  27.7 us
    dot_general x1, matrix products, local(): lax.dot_general(grad_gate, gate_mat, transposed, preferred_element_type=j...  7.57 us
    dot_general x1, matrix products, local(): lax.dot_general(grad_up, up_mat, transposed, preferred_element_type=jnp.f...  7 us
  transfers between devices with their start and end apart: 6, of which 6 were waited for; matrix products, arithmetic and copies ran while one was open for 10% of the time, Pallas kernels for 0%

profile of v1, /device:TPU:11, one launch (start us, length us, event | category | flops | bytes accessed | tf_op | source)
XLA Modules:
  0.0 331.4 jit_solution(2727360676831782622)
XLA Ops:
  7.2 0.8 copy.28
  8.0 0.1 eq.44
  8.2 4.5 %reduce-window.6 = s32[16,8,128]{2,1,0:T(8,128)S(1)} reduce-window(s32[16,8,128]{2,1,0:T(8,128)S(1)} %fusion.48, s32[]{:T(128)} %constant.13.clone.1), window={size=1x1x128 pad=0_0x0_0x127_0}, to_apply=%region_0.0 | reduce-window | flops 2080768 | bytes 131076 | tf_op jit(solution)/shard_map/reduce-window
  12.8 0.1 copy.30
  13.3 0.7 multiply_add_fusion
  14.0 2.3 select_reduce_fusion
  16.4 1.9 multiply_convert_fusion
  18.3 6.7 %all-to-all-start.2 = ((bf16[16,32,1792]{2,1,0:T(8,128)(2,1)}), bf16[16,32,1792]{2,1,0:T(8,128)(2,1)S(1)}, u32[]{:S(2)}, u32[]{:S(2)}) async-start(bf16[16,32,1792]{2,1,0:T(8,128)(2,1)} %bitcast.10), calls=%async_computation.2 | async-start | bytes 3670016 | tf_op jit(solution)/shard_map/all_to_all | solution.py:47
  25.0 1.8 convolution_convert_fusion.1
  26.8 39.9 %all-to-all-done.2 = bf16[16,32,1792]{2,1,0:T(8,128)(2,1)S(1)} async-done(((bf16[16,32,1792]{2,1,0:T(8,128)(2,1)}), bf16[16,32,1792]{2,1,0:T(8,128)(2,1)S(1)}, u32[]{:S(2)}, u32[]{:S(2)}) %all-to-all-start.2) | async-done | bytes 1835040 | tf_op jit(solution)/shard_map/all_to_all | solution.py:47
  66.8 4.8 %all-to-all-start = ((bf16[16,32,1792]{2,1,0:T(8,128)(2,1)}), bf16[16,32,1792]{2,1,0:T(8,128)(2,1)}, u32[]{:S(2)}, u32[]{:S(2)}) async-start(bf16[16,32,1792]{2,1,0:T(8,128)(2,1)} %bitcast.2), calls=%async_computation | async-start | bytes 3670016 | tf_op jit(solution)/shard_map/all_to_all | solution.py:32
  71.6 5.1 %fusion.39 = bf16[512,1024]{1,0:T(8,128)(2,1)} fusion(bf16[512,1792]{1,0:T(8,128)(2,1)S(1)} %bitcast.72, bf16[1,1024,1792]{2,1,0:T(8,128)(2,1)} %param.12), kind=kOutput, calls=%fused_computation.46 | convolution fusion | flops 1879572480 | bytes 6553600 | tf_op jit(solution)/shard_map/dot_general | solution.py:49
  76.7 36.7 %all-to-all-done = bf16[16,32,1792]{2,1,0:T(8,128)(2,1)} async-done(((bf16[16,32,1792]{2,1,0:T(8,128)(2,1)}), bf16[16,32,1792]{2,1,0:T(8,128)(2,1)}, u32[]{:S(2)}, u32[]{:S(2)}) %all-to-all-start) | async-done | bytes 1835040 | tf_op jit(solution)/shard_map/all_to_all | solution.py:32
  113.4 5.6 %fusion.33 = bf16[512,1024]{1,0:T(8,128)(2,1)} fusion(bf16[512,1792]{1,0:T(8,128)(2,1)} %bitcast.3, bf16[1,1792,1024]{2,1,0:T(8,128)(2,1)} %param.10), kind=kOutput, calls=%fused_computation.44 | convolution fusion | flops 1879572480 | bytes 6553600 | tf_op jit(solution)/shard_map/dot_general | solution.py:34
  119.1 0.2 all-gather.3.cloned.1.call-start
  119.3 5.7 %fusion.36 = bf16[512,1024]{1,0:T(8,128)(2,1)} fusion(bf16[512,1792]{1,0:T(8,128)(2,1)} %bitcast.3, bf16[1,1792,1024]{2,1,0:T(8,128)(2,1)} %param.11), kind=kOutput, calls=%fused_computation.45 | convolution fusion | flops 1879572480 | bytes 6553600 | tf_op jit(solution)/shard_map/dot_general | solution.py:35
  125.1 56.4 %all-reduce.3.cloned.1.call-done = (bf16[512,1024]{1,0:T(8,128)(2,1)}, bf16[512,1024]{1,0:T(8,128)(2,1)}) async-done(((bf16[512,1024]{1,0:T(8,128)(2,1)}, bf16[512,1024]{1,0:T(8,128)(2,1)}), (bf16[512,1024]{1,0:T(8,128)(2,1)}, bf16[512,1024]{1,0:T(8,128)(2,1)})) %all-reduce.3.cloned.1.call-update) | async-done | bytes 2097168 | tf_op jit(solution)/shard_map/psum | solution.py:36
  181.5 7.0 %fusion.7 = f32[512,1792]{1,0:T(8,128)} fusion(bf16[1,1792,1024]{2,1,0:T(8,128)(2,1)} %param.11, bf16[512,1024]{1,0:T(8,128)(2,1)} %get-tuple-element.6, bf16[512,1024]{1,0:T(8,128)(2,1)} %get-tuple-element.5), kind=kOutput, calls=%fused_computation.9 | convolution fusion | flops 1883242496 | bytes 9437184 | tf_op jit(solution)/shard_map/dot_general | solution.py:55
  188.5 27.7 %all-gather.3.cloned.1.call-done = bf16[1024,1024]{1,0:T(8,128)(2,1)} async-done(((bf16[512,1024]{1,0:T(8,128)(2,1)}), bf16[1024,1024]{1,0:T(8,128)(2,1)}) %all-gather.3.cloned.1.call-update) | async-done | bytes 2097168 | tf_op jit(solution)/shard_map/all_gather | solution.py:37
  216.2 2.2 reduce_sum.44
  218.3 7.6 %add_convert_fusion = bf16[512,1792]{1,0:T(8,128)(2,1)} fusion(f32[512,1792]{1,0:T(8,128)} %fusion.7, bf16[1,1792,1024]{2,1,0:T(8,128)(2,1)} %param.10, bf16[512,1024]{1,0:T(8,128)(2,1)S(1)} %reduce_sum.44, bf16[512,1024]{1,0:T(8,128)(2,1)} %get-tuple-element.6, bf16[512,1024]{1,0:T(8,128)(2,1)S(1)} %copy-done.5), kind=kOutput, calls=%fused_computation.17 | convolution fusion | flops 1887698944 | bytes 12320768 | tf_op jit(solution)/shard_map/dot_general | solution.py:54
  225.9 6.5 %all-to-all-start.3 = ((bf16[16,32,1792]{2,1,0:T(8,128)(2,1)}), bf16[16,32,1792]{2,1,0:T(8,128)(2,1)S(1)}, u32[]{:S(2)}, u32[]{:S(2)}) async-start(bf16[16,32,1792]{2,1,0:T(8,128)(2,1)} %bitcast.75), calls=%async_computation.3 | async-start | bytes 3670016 | tf_op jit(solution)/shard_map/all_to_all | solution.py:63
  232.4 6.1 %fusion.18 = bf16[512,1792]{1,0:T(8,128)(2,1)} fusion(bf16[1,1024,1792]{2,1,0:T(8,128)(2,1)} %param.12, bf16[512,1024]{1,0:T(8,128)(2,1)S(1)} %reduce_sum.44, bf16[512,1024]{1,0:T(8,128)(2,1)} %get-tuple-element.5), kind=kOutput, calls=%fused_computation.23 | convolution fusion | flops 1884160000 | bytes 7602176 | tf_op jit(solution)/shard_map/dot_general | solution.py:39
  238.5 35.7 %all-to-all-done.3 = bf16[16,32,1792]{2,1,0:T(8,128)(2,1)S(1)} async-done(((bf16[16,32,1792]{2,1,0:T(8,128)(2,1)}), bf16[16,32,1792]{2,1,0:T(8,128)(2,1)S(1)}, u32[]{:S(2)}, u32[]{:S(2)}) %all-to-all-start.3) | async-done | bytes 1835040 | tf_op jit(solution)/shard_map/all_to_all | solution.py:63
  274.2 1.3 copy-done.1
  275.5 4.8 %all-to-all-start.1 = ((bf16[16,32,1792]{2,1,0:T(8,128)(2,1)}), bf16[16,32,1792]{2,1,0:T(8,128)(2,1)S(1)}, u32[]{:S(2)}, u32[]{:S(2)}) async-start(bf16[16,32,1792]{2,1,0:T(8,128)(2,1)} %bitcast.74), calls=%async_computation.1 | async-start | bytes 3670016 | tf_op jit(solution)/shard_map/all_to_all | solution.py:46
  280.3 6.0 %fusion.15 = bf16[1,1024,1792]{2,1,0:T(8,128)(2,1)} fusion(bf16[512,1792]{1,0:T(8,128)(2,1)} %bitcast.73, bf16[512,1024]{1,0:T(8,128)(2,1)S(1)} %reduce_sum.44, bf16[512,1024]{1,0:T(8,128)(2,1)} %get-tuple-element.5), kind=kOutput, calls=%fused_computation.19 | convolution fusion | flops 1885077504 | bytes 7602176 | tf_op jit(solution)/shard_map/dot_general | solution.py:59
  286.3 1.2 convolution_convert_fusion.2
  287.5 34.6 %all-to-all-done.1 = bf16[16,32,1792]{2,1,0:T(8,128)(2,1)S(1)} async-done(((bf16[16,32,1792]{2,1,0:T(8,128)(2,1)}), bf16[16,32,1792]{2,1,0:T(8,128)(2,1)S(1)}, u32[]{:S(2)}, u32[]{:S(2)}) %all-to-all-start.1) | async-done | bytes 1835040 | tf_op jit(solution)/shard_map/all_to_all | solution.py:46
  322.1 0.4 fusion.1
  322.5 0.4 fusion.53
  322.9 1.7 fusion.21
  (24 shorter events, 0.6 us)
Async XLA Ops:
  7.2 9.2 %copy-start = (bf16[128,1792]{1,0:T(8,128)(2,1)S(1)}, bf16[128,1792]{1,0:T(8,128)(2,1)}, u32[]{:S(2)}) copy-start(bf16[128,1792]{1,0:T(8,128)(2,1)} %param.13) | copy-start | bytes 1376260
  18.3 6.7 %copy-start.4 = (bf16[128,1792]{1,0:T(8,128)(2,1)S(1)}, bf16[128,1792]{1,0:T(8,128)(2,1)}, u32[]{:S(2)}) copy-start(bf16[128,1792]{1,0:T(8,128)(2,1)} %param.7) | copy-start | bytes 1376260
  18.3 48.5 %all-to-all-start.2 = ((bf16[16,32,1792]{2,1,0:T(8,128)(2,1)}), bf16[16,32,1792]{2,1,0:T(8,128)(2,1)S(1)}, u32[]{:S(2)}, u32[]{:S(2)}) async-start(bf16[16,32,1792]{2,1,0:T(8,128)(2,1)} %bitcast.10), calls=%async_computation.2 | async-start | bytes 3670016 | tf_op jit(solution)/shard_map/all_to_all | solution.py:47
  66.8 9.9 %copy-start.3 = (bf16[16,32,1792]{2,1,0:T(8,128)(2,1)}, bf16[16,32,1792]{2,1,0:T(8,128)(2,1)S(1)}, u32[]{:S(2)}) copy-start(bf16[16,32,1792]{2,1,0:T(8,128)(2,1)S(1)} %all-to-all-done.2) | copy-start | bytes 5505028
  66.8 46.7 %all-to-all-start = ((bf16[16,32,1792]{2,1,0:T(8,128)(2,1)}), bf16[16,32,1792]{2,1,0:T(8,128)(2,1)}, u32[]{:S(2)}, u32[]{:S(2)}) async-start(bf16[16,32,1792]{2,1,0:T(8,128)(2,1)} %bitcast.2), calls=%async_computation | async-start | bytes 3670016 | tf_op jit(solution)/shard_map/all_to_all | solution.py:32
  71.5 110.0 %all-reduce.3.cloned.1.call-start = ((), (), s32[]{:S(2)}) async-start(), calls=%async_computation.5 | async-start | bytes 4194304 | tf_op jit(solution)/shard_map/psum | solution.py:36
  119.1 97.1 %all-gather.3.cloned.1.call-start = ((), (), s32[]{:S(2)}) async-start(), calls=%async_computation.4 | async-start | bytes 3145728 | tf_op jit(solution)/shard_map/all_gather | solution.py:37
  188.5 29.8 %copy-start.5 = (bf16[512,1024]{1,0:T(8,128)(2,1)S(1)}, bf16[512,1024]{1,0:T(8,128)(2,1)}, u32[]{:S(2)}) copy-start(bf16[512,1024]{1,0:T(8,128)(2,1)} %get-tuple-element.5) | copy-start | bytes 3145732
  225.9 48.3 %all-to-all-start.3 = ((bf16[16,32,1792]{2,1,0:T(8,128)(2,1)}), bf16[16,32,1792]{2,1,0:T(8,128)(2,1)S(1)}, u32[]{:S(2)}, u32[]{:S(2)}) async-start(bf16[16,32,1792]{2,1,0:T(8,128)(2,1)} %bitcast.75), calls=%async_computation.3 | async-start | bytes 3670016 | tf_op jit(solution)/shard_map/all_to_all | solution.py:63
  274.2 1.3 copy-start.1
  275.5 46.6 %all-to-all-start.1 = ((bf16[16,32,1792]{2,1,0:T(8,128)(2,1)}), bf16[16,32,1792]{2,1,0:T(8,128)(2,1)S(1)}, u32[]{:S(2)}, u32[]{:S(2)}) async-start(bf16[16,32,1792]{2,1,0:T(8,128)(2,1)} %bitcast.74), calls=%async_computation.1 | async-start | bytes 3670016 | tf_op jit(solution)/shard_map/all_to_all | solution.py:46
  280.3 6.0 %copy-start.2 = (bf16[16,32,1792]{2,1,0:T(8,128)(2,1)S(1)}, bf16[16,32,1792]{2,1,0:T(8,128)(2,1)}, u32[]{:S(2)}) copy-start(bf16[16,32,1792]{2,1,0:T(8,128)(2,1)} %copy-done.1) | copy-start | bytes 5505028
Sparse Core Ops, SparseCore 0:
  119.2 62.2 all-reduce.2
  183.0 33.0 all-gather.2
